TPU v7x, 32 devices: a whole 2x2x4 slice. The times are simulated.
32 devices in a mesh: sec: 4 (over y, x), col: 8 (over z, core).
Axes of the slice: x: 2, y: 2, z: 4, core: 2. Of those that a mesh axis runs over, the one named last changes fastest.
Arguments:
- matrix_rows: float32 [4096, 16384], P('sec', 'col'), may hold values from -6 to 6
- factor_bank: float32 [4, 8, 512, 512], P(None, 'sec', 'col'), may hold values from -1 to 1, as said below
- owner_table: int32 [4, 8, 8], P(None, 'sec'), may hold values from 0 to 7, each once within a row
Outputs:
- updated: float32 [4096, 16384], P('sec', 'col')
Inputs may be any that keep to these rules, and one draw needn't show every extreme that they name: `factor_bank`: each factor G[r,k] is orthogonal. `owner_table`: for each round and section the list names every row block once.
All inputs are finite; a program needn't handle non-finite values.
Results may differ from a plain program's by a relative error of at most 0.00014.
Values sent between devices are 32-bit elements; how exact they have to be, the bound alone decides.
A program may use at most 128 MiB of HBM per device.

v0:
```python
import functools

import jax
import jax.numpy as jnp
from jax import lax
from jax.experimental import pallas as pl
from jax.experimental.pallas import tpu as pltpu
from jax.sharding import PartitionSpec as P

ROUNDS = 4
WIDTH = 256
PIECES = 2


def unit_order(sections):
    order = []
    for number in range(ROUNDS):
        ks = list(range(sections))
        if number % 2 == 0:
            ks = ks[::-1]
        order += [(number, k) for k in ks]
    return order


def strip_kernel(nsec, count, chunks, width, *refs):
    table_ref, x_ref, bank_ref, out_ref = refs[:4]
    xs, sa, sb, rs, ghi, glo = refs[4:10]
    sections = bank_ref.shape[1]
    order = unit_order(sections)
    units = len(order)
    held = refs[10 : 10 + units]
    (x_sems, o_sems, own_sems, up_sems, down_sems, piece_sems, far_sems, relay_sems, row_sems) = refs[10 + units :]

    extent = bank_ref.shape[3]
    half = extent // 2
    rows = bank_ref.shape[2]
    local_rows = sections * extent
    chips = count // 2
    sec = lax.axis_index("sec")
    me = lax.axis_index("col")
    chip, core = me // 2, me % 2
    partner = chip * 2 + 1 - core
    after = lax.rem(sec + 1, nsec)
    before = lax.rem(sec + nsec - 1, nsec)

    def columns(c):
        return pl.ds(pl.multiple_of(c * width, width), width)

    def load(c, k):
        return pltpu.make_async_copy(
            x_ref.at[pl.ds(k * extent, extent), columns(c)],
            xs.at[c, pl.ds(half + k * extent, extent)],
            x_sems.at[k, c],
        )

    def own(u):
        number, k = order[u]
        return pltpu.make_async_copy(bank_ref.at[number, k], held[u].at[core, chip], own_sems.at[u])

    for k in range(sections - 1, -1, -1):
        lax.fori_loop(0, chunks, lambda c, _, k=k: (load(c, k).start(), 0)[1], 0)
    for u in range(units):
        own(u).start()

    barrier = pltpu.get_barrier_semaphore()

    def greet(target):
        pl.semaphore_signal(barrier, inc=1, device_id=target, device_id_type=pl.DeviceIdType.MESH)

    greet({"col": partner})
    for d in range(1, chips):
        greet({"col": lax.rem(chip + d, chips) * 2 + core})
    greet({"sec": after})
    greet({"sec": before})
    pl.semaphore_wait(barrier, chips + 2)

    def remote(src, dst, sems, at, target):
        return pltpu.make_async_remote_copy(
            src_ref=src,
            dst_ref=dst,
            send_sem=sems.at[(0, *at)],
            recv_sem=sems.at[(1, *at)],
            device_id=target,
            device_id_type=pl.DeviceIdType.MESH,
        )

    part = rows // PIECES
    first_number, first_k = order[0]

    def piece(p):
        return pl.ds(p * part, part)

    def pass_up(src, slot, step, p):
        return remote(src, held[0].at[core, slot, piece(p)], up_sems, (step, p), {"col": (chip + 1) * 2 + core})

    def pass_down(src, slot, step, p):
        return remote(src, held[0].at[core, slot, piece(p)], down_sems, (step, p), {"col": (chip - 1) * 2 + core})

    def pass_pair(src, slot, step, p):
        return remote(src, held[0].at[core, slot, piece(p)], piece_sems, (step, p), {"col": partner})

    def own_piece(p):
        return bank_ref.at[first_number, first_k, piece(p)]

    has_up, has_down = chip + 1 < chips, chip > 0
    for p in range(PIECES):
        pl.when(has_up)(lambda p=p: pass_up(own_piece(p), chip, 0, p).start())
        pl.when(has_down)(lambda p=p: pass_down(own_piece(p), chip, 0, p).start())
    for p in range(PIECES):
        pass_pair(own_piece(p), chip, 0, p).start()
    for step in range(chips - 1):
        low, high = chip - 1 - step, chip + 1 + step
        for p in range(PIECES):

            @pl.when(low >= 0)
            def _(step=step, p=p, low=low):
                src = held[0].at[core, low, piece(p)]
                pass_up(src, low, step, p).wait_recv()
                if step + 1 < chips - 1:
                    pl.when(has_up)(lambda: pass_up(src, low, step + 1, p).start())
                pass_pair(src, low, 1 + step, p).start()

            @pl.when(high < chips)
            def _(step=step, p=p, high=high):
                src = held[0].at[core, high, piece(p)]
                pass_down(src, high, step, p).wait_recv()
                if step + 1 < chips - 1:
                    pl.when(has_down)(lambda: pass_down(src, high, step + 1, p).start())
                pass_pair(src, high, chips + step, p).start()

    def far(u, d):
        number, k = order[u]
        return remote(
            bank_ref.at[number, k],
            held[u].at[core, chip],
            far_sems,
            (u, d - 1),
            {"col": lax.rem(chip + d, chips) * 2 + core},
        )

    def far_arrival(u, d):
        return remote(
            bank_ref.at[order[u]],
            held[u].at[core, lax.rem(chip + chips - d, chips)],
            far_sems,
            (u, d - 1),
            {"col": partner},
        )

    def relay(u, side):
        return remote(held[u].at[side], held[u].at[side], relay_sems, (u,), {"col": partner})

    def order_rows(u):
        number, k = order[u]
        for b in range(count):
            place = jnp.int32(0)
            for c in range(count):
                place = jnp.where(table_ref[number, k, c] == b, c, place)
            block = held[u][place % 2, place // 2]
            high = block.astype(jnp.bfloat16)
            ghi[u, b * rows : (b + 1) * rows, :] = high
            glo[u, b * rows : (b + 1) * rows, :] = (block - high.astype(jnp.float32)).astype(jnp.bfloat16)

    own(0).wait()
    for step in range(chips - 1):
        low, high = chip - 1 - step, chip + 1 + step
        for p in range(PIECES):
            pl.when(low >= 0)(
                lambda: pass_pair(held[0].at[1 - core, low, piece(p)], low, 1 + step, p).wait_recv()
            )
            pl.when(high < chips)(
                lambda: pass_pair(held[0].at[1 - core, high, piece(p)], high, chips + step, p).wait_recv()
            )
    for p in range(PIECES):
        pass_pair(held[0].at[1 - core, chip, piece(p)], chip, 0, p).wait_recv()
    order_rows(0)

    def receive(u):
        for d in range(1, chips):
            far_arrival(u, d).wait_recv()
        own(u).wait()
        relay(u, core).start()
        relay(u, 1 - core).wait_recv()
        order_rows(u)

    def split(value):
        high = value.astype(jnp.bfloat16)
        return high, (value - high.astype(jnp.float32)).astype(jnp.bfloat16)

    def product(u, begin, size, parts):
        high, low = parts
        a, b = ghi[u, begin : begin + size, :], glo[u, begin : begin + size, :]
        dot = functools.partial(jnp.dot, preferred_element_type=jnp.float32)
        return dot(a, high) + (dot(a, low) + dot(b, high))

    index = {pair: u for u, pair in enumerate(order)}
    top = half + local_rows

    def forward(c, which, buf):
        return remote(
            buf.at[c, pl.ds(top - half, half)], buf.at[c, pl.ds(0, half)], row_sems, (which, c), {"sec": after}
        )

    def back_first(c):
        return remote(rs.at[c], sb.at[c, pl.ds(local_rows - half, half)], row_sems, (1, c), {"sec": before})

    def back_last(c):
        return remote(
            sa.at[c, pl.ds(0, half)],
            out_ref.at[pl.ds(local_rows - half, half), columns(c)],
            row_sems,
            (3, c),
            {"sec": before},
        )

    def each_chunk(body):
        lax.fori_loop(0, chunks, lambda c, _: (body(c), 0)[1], 0)

    last = sections - 1

    def begin(c):
        load(c, last).wait()
        parts = split(xs[c, half + last * extent : top])
        u = index[0, last]
        sa[c, top - half : top] = product(u, half, half, parts)
        forward(c, 0, sa).start()
        sa[c, half + last * extent : top - half] = product(u, 0, half, parts)

    each_chunk(begin)
    for u in range(1, units):
        for d in range(1, chips):
            far(u, d).start()

    for k in range(last - 1, -1, -1):
        receive(index[0, k])

        def inner(c, k=k):
            load(c, k).wait()
            at = half + k * extent
            parts = split(xs[c, at : at + extent])
            sa[c, at : at + extent] = product(index[0, k], 0, extent, parts)

        each_chunk(inner)

    receive(index[1, 0])

    def straddle(c):
        forward(c, 0, sa).wait_recv()
        parts = split(sa[c, 0:extent])
        u = index[1, 0]
        rs[c] = product(u, 0, half, parts)
        back_first(c).start()
        sb[c, 0:half] = product(u, half, half, parts)

    each_chunk(straddle)
    for k in range(1, sections):
        receive(index[1, k])

        def inner(c, k=k):
            parts = split(sa[c, k * extent : (k + 1) * extent])
            sb[c, k * extent - half : (k + 1) * extent - half] = product(index[1, k], 0, extent, parts)

        each_chunk(inner)

    for k in range(last, -1, -1):
        receive(index[2, k])

    def middle(c):
        back_first(c).wait_recv()
        parts = split(sb[c, last * extent : local_rows])
        u = index[2, last]
        xs[c, top - half : top] = product(u, half, half, parts)
        forward(c, 2, xs).start()
        xs[c, half + last * extent : top - half] = product(u, 0, half, parts)
        for k in range(last):
            at = half + k * extent
            parts = split(sb[c, k * extent : (k + 1) * extent])
            xs[c, at : at + extent] = product(index[2, k], 0, extent, parts)

    each_chunk(middle)

    for k in range(sections):
        receive(index[3, k])

    def store(c):
        return pltpu.make_async_copy(
            sa.at[c, pl.ds(half, local_rows - half)],
            out_ref.at[pl.ds(0, local_rows - half), columns(c)],
            o_sems.at[c],
        )

    def finish(c):
        forward(c, 2, xs).wait_recv()
        forward(c, 0, sa).wait_send()
        parts = split(xs[c, 0:extent])
        u = index[3, 0]
        sa[c, 0:half] = product(u, 0, half, parts)
        back_last(c).start()
        sa[c, half:extent] = product(u, half, half, parts)
        for k in range(1, sections):
            parts = split(xs[c, k * extent : (k + 1) * extent])
            sa[c, k * extent : (k + 1) * extent] = product(index[3, k], 0, extent, parts)
        store(c).start()

    each_chunk(finish)

    def drain(c):
        back_first(c).wait_send()
        forward(c, 2, xs).wait_send()
        store(c).wait()
        back_last(c).wait_send()
        back_last(c).wait_recv()

    for p in range(PIECES):
        pass_pair(own_piece(p), chip, 0, p).wait_send()
        pl.when(has_up)(lambda p=p: pass_up(own_piece(p), chip, 0, p).wait_send())
        pl.when(has_down)(lambda p=p: pass_down(own_piece(p), chip, 0, p).wait_send())
        for step in range(chips - 1):
            low, high = chip - 1 - step, chip + 1 + step

            @pl.when(low >= 0)
            def _():
                if step + 1 < chips - 1:
                    pl.when(has_up)(lambda: pass_up(held[0].at[core, low, piece(p)], low, step + 1, p).wait_send())
                pass_pair(held[0].at[core, low, piece(p)], low, 1 + step, p).wait_send()

            @pl.when(high < chips)
            def _():
                if step + 1 < chips - 1:
                    pl.when(has_down)(
                        lambda: pass_down(held[0].at[core, high, piece(p)], high, step + 1, p).wait_send()
                    )
                pass_pair(held[0].at[core, high, piece(p)], high, chips + step, p).wait_send()

    for u in range(1, units):
        for d in range(1, chips):
            far(u, d).wait_send()
        relay(u, core).wait_send()
    each_chunk(drain)


def local(matrix_rows, factor_bank, owner_table):
    nsec, count = lax.axis_size("sec"), lax.axis_size("col")
    sections, rows, extent = factor_bank.shape[1:]
    local_rows, columns = matrix_rows.shape
    half, chips = extent // 2, count // 2
    width = WIDTH if columns % WIDTH == 0 else columns
    chunks = columns // width
    units = ROUNDS * sections
    f32, bf16, dma = jnp.float32, jnp.bfloat16, pltpu.SemaphoreType.DMA
    return pl.pallas_call(
        functools.partial(strip_kernel, nsec, count, chunks, width),
        out_shape=jax.ShapeDtypeStruct(matrix_rows.shape, matrix_rows.dtype),
        in_specs=[
            pl.BlockSpec(memory_space=pltpu.SMEM),
            pl.BlockSpec(memory_space=pl.ANY),
            pl.BlockSpec(memory_space=pl.ANY),
        ],
        out_specs=pl.BlockSpec(memory_space=pl.ANY),
        scratch_shapes=[
            pltpu.VMEM((chunks, half + local_rows, width), f32),
            pltpu.VMEM((chunks, half + local_rows, width), f32),
            pltpu.VMEM((chunks, local_rows, width), f32),
            pltpu.VMEM((chunks, half, width), f32),
            pltpu.VMEM((units, extent, extent), bf16),
            pltpu.VMEM((units, extent, extent), bf16),
            *[pltpu.VMEM((2, chips, rows, extent), f32) for _ in range(units)],
            dma((sections, chunks)),
            dma((chunks,)),
            dma((units,)),
            dma((2, chips - 1, PIECES)),
            dma((2, chips - 1, PIECES)),
            dma((2, 2 * chips - 1, PIECES)),
            dma((2, units, chips - 1)),
            dma((2, units)),
            dma((2, 4, chunks)),
        ],
        compiler_params=pltpu.CompilerParams(
            collective_id=0, has_side_effects=True, vmem_limit_bytes=60 << 20
        ),
        name="strip",
    )(owner_table, matrix_rows, factor_bank)


def solution(mesh):
    in_specs = (P("sec", "col"), P(None, "sec", "col", None), P(None, "sec", None))
    out_specs = P("sec", "col")
    return jax.shard_map(local, mesh=mesh, in_specs=in_specs, out_specs=out_specs, check_vma=False)
```

profile of v0, /device:TPU:0, one launch (start us, length us, event | category | flops | bytes accessed | tf_op | source)
XLA Modules:
  0.0 209.4 jit_solution(10550469215013609802)
XLA Ops:
  0.0 201.5 %strip.1 = f32[1024,2048]{1,0:T(8,128)} custom-call(s32[4,2,8]{2,1,0:T(2,128)} %refs_0_.1, f32[1024,2048]{1,0:T(8,128)} %refs_1_.1, f32[4,2,64,512]{3,2,1,0:T(8,128)} %refs_2_.1), custom_call_target="tpu_custom_call" | custom-call | tf_op jit(solution)/shard_map/strip/pallas_call | solution.py:351
  201.5 7.9 %copy.5 = f32[1024,2048]{1,0:T(8,128)} copy(f32[1024,2048]{1,0:T(8,128)} %strip.1) | data formatting | bytes 16777216
where the time goes:
time: 210 us; the launch traced here: 209 us
  Pallas kernels  201 us (96%)
  local copies, waits for them, and re-layouts  7.89 us (4%)
    pallas_call x1, Pallas kernels, local(): pl.pallas_call(functools.partial(strip_kernel, nsec, count, chunks, width...  201 us
    unnamed x1, local copies, waits for them, and re-layouts  7.89 us

commit v1 on v0

--- a/solution.py
+++ b/solution.py
@@ -29,7 +29,7 @@
     order = unit_order(sections)
     units = len(order)
     held = refs[10 : 10 + units]
-    (x_sems, o_sems, own_sems, up_sems, down_sems, piece_sems, far_sems, relay_sems, row_sems) = refs[10 + units :]
+    (x_sems, own_sems, up_sems, down_sems, piece_sems, far_sems, relay_sems, row_sems) = refs[10 + units :]
 
     extent = bank_ref.shape[3]
     half = extent // 2
@@ -282,32 +282,25 @@
     for k in range(sections):
         receive(index[3, k])
 
-    def store(c):
-        return pltpu.make_async_copy(
-            sa.at[c, pl.ds(half, local_rows - half)],
-            out_ref.at[pl.ds(0, local_rows - half), columns(c)],
-            o_sems.at[c],
-        )
-
     def finish(c):
         forward(c, 2, xs).wait_recv()
-        forward(c, 0, sa).wait_send()
         parts = split(xs[c, 0:extent])
         u = index[3, 0]
         sa[c, 0:half] = product(u, 0, half, parts)
         back_last(c).start()
-        sa[c, half:extent] = product(u, half, half, parts)
+        out_ref[0:half, columns(c)] = product(u, half, half, parts)
         for k in range(1, sections):
             parts = split(xs[c, k * extent : (k + 1) * extent])
-            sa[c, k * extent : (k + 1) * extent] = product(index[3, k], 0, extent, parts)
-        store(c).start()
+            out_ref[k * extent - half : (k + 1) * extent - half, columns(c)] = product(
+                index[3, k], 0, extent, parts
+            )
 
     each_chunk(finish)
 
     def drain(c):
+        forward(c, 0, sa).wait_send()
         back_first(c).wait_send()
         forward(c, 2, xs).wait_send()
-        store(c).wait()
         back_last(c).wait_send()
         back_last(c).wait_recv()
 
@@ -350,13 +343,13 @@
     f32, bf16, dma = jnp.float32, jnp.bfloat16, pltpu.SemaphoreType.DMA
     return pl.pallas_call(
         functools.partial(strip_kernel, nsec, count, chunks, width),
-        out_shape=jax.ShapeDtypeStruct(matrix_rows.shape, matrix_rows.dtype),
+        out_shape=pltpu.VMEM(matrix_rows.shape, matrix_rows.dtype),
         in_specs=[
             pl.BlockSpec(memory_space=pltpu.SMEM),
             pl.BlockSpec(memory_space=pl.ANY),
             pl.BlockSpec(memory_space=pl.ANY),
         ],
-        out_specs=pl.BlockSpec(memory_space=pl.ANY),
+        out_specs=pl.BlockSpec(memory_space=pltpu.VMEM),
         scratch_shapes=[
             pltpu.VMEM((chunks, half + local_rows, width), f32),
             pltpu.VMEM((chunks, half + local_rows, width), f32),
@@ -366,7 +359,6 @@
             pltpu.VMEM((units, extent, extent), bf16),
             *[pltpu.VMEM((2, chips, rows, extent), f32) for _ in range(units)],
             dma((sections, chunks)),
-            dma((chunks,)),
             dma((units,)),
             dma((2, chips - 1, PIECES)),
             dma((2, chips - 1, PIECES)),
@@ -376,7 +368,7 @@
             dma((2, 4, chunks)),
         ],
         compiler_params=pltpu.CompilerParams(
-            collective_id=0, has_side_effects=True, vmem_limit_bytes=60 << 20
+            collective_id=0, has_side_effects=True, vmem_limit_bytes=50 << 20
         ),
         name="strip",
     )(owner_table, matrix_rows, factor_bank)

time: 210 us -> 205 us (0.976)
  local copies, waits for them, and re-layouts: 7.89 us -> 3.4 us
    unnamed x1, local copies, waits for them, and re-layouts: 7.89 us -> 3.4 us
where the time goes in v1:
time: 205 us
  Pallas kernels  201 us (98%)
  local copies, waits for them, and re-layouts  3.4 us (2%)
    pallas_call x1, Pallas kernels, local(): pl.pallas_call(functools.partial(strip_kernel, nsec, count, chunks, width...  201 us

profile of v1, /device:TPU:0, one launch (start us, length us, event | category | flops | bytes accessed | tf_op | source)
XLA Modules:
  0.0 204.7 jit_solution(17895195724902929404)
XLA Ops:
  0.0 201.3 %strip.1 = f32[1024,2048]{1,0:T(8,128)S(1)} custom-call(s32[4,2,8]{2,1,0:T(2,128)} %refs_0_.1, f32[1024,2048]{1,0:T(8,128)} %refs_1_.1, f32[4,2,64,512]{3,2,1,0:T(8,128)} %refs_2_.1), custom_call_target="tpu_custom_call" | custom-call | tf_op jit(solution)/shard_map/strip/pallas_call | solution.py:344
  201.3 3.4 %copy.5 = f32[1024,2048]{1,0:T(8,128)} copy(f32[1024,2048]{1,0:T(8,128)S(1)} %strip.1) | data formatting | bytes 16777216

commit v2 on v1

--- a/solution.py
+++ b/solution.py
@@ -67,12 +67,13 @@
     def greet(target):
         pl.semaphore_signal(barrier, inc=1, device_id=target, device_id_type=pl.DeviceIdType.MESH)
 
-    greet({"col": partner})
-    for d in range(1, chips):
-        greet({"col": lax.rem(chip + d, chips) * 2 + core})
+    has_up, has_down = chip + 1 < chips, chip > 0
     greet({"sec": after})
     greet({"sec": before})
-    pl.semaphore_wait(barrier, chips + 2)
+    greet({"col": partner})
+    pl.when(has_up)(lambda: greet({"col": (chip + 1) * 2 + core}))
+    pl.when(has_down)(lambda: greet({"col": (chip - 1) * 2 + core}))
+    pl.semaphore_wait(barrier, 3 + has_up.astype(jnp.int32) + has_down.astype(jnp.int32))
 
     def remote(src, dst, sems, at, target):
         return pltpu.make_async_remote_copy(
@@ -102,7 +103,6 @@
     def own_piece(p):
         return bank_ref.at[first_number, first_k, piece(p)]
 
-    has_up, has_down = chip + 1 < chips, chip > 0
     for p in range(PIECES):
         pl.when(has_up)(lambda p=p: pass_up(own_piece(p), chip, 0, p).start())
         pl.when(has_down)(lambda p=p: pass_down(own_piece(p), chip, 0, p).start())

time: 205 us -> 205 us (level)
  no operation moved by 1% of the time
where the time goes in v2:
time: 205 us
  Pallas kernels  201 us (98%)
  local copies, waits for them, and re-layouts  3.4 us (2%)
    pallas_call x1, Pallas kernels, local(): pl.pallas_call(functools.partial(strip_kernel, nsec, count, chunks, width...  201 us

profile of v2, /device:TPU:0, one launch (start us, length us, event | category | flops | bytes accessed | tf_op | source)
XLA Modules:
  0.0 204.7 jit_solution(7243133184175250359)
XLA Ops:
  0.0 201.3 %strip.1 = f32[1024,2048]{1,0:T(8,128)S(1)} custom-call(s32[4,2,8]{2,1,0:T(2,128)} %refs_0_.1, f32[1024,2048]{1,0:T(8,128)} %refs_1_.1, f32[4,2,64,512]{3,2,1,0:T(8,128)} %refs_2_.1), custom_call_target="tpu_custom_call" | custom-call | tf_op jit(solution)/shard_map/strip/pallas_call | solution.py:344
  201.3 3.4 %copy.5 = f32[1024,2048]{1,0:T(8,128)} copy(f32[1024,2048]{1,0:T(8,128)S(1)} %strip.1) | data formatting | bytes 16777216

commit v3 on v2

--- a/solution.py
+++ b/solution.py
@@ -24,12 +24,12 @@
 
 def strip_kernel(nsec, count, chunks, width, *refs):
     table_ref, x_ref, bank_ref, out_ref = refs[:4]
-    xs, sa, sb, rs, ghi, glo = refs[4:10]
+    xs, sa, sb, rs, ghi, glo, raw, names, named, ahi, alo = refs[4:15]
     sections = bank_ref.shape[1]
     order = unit_order(sections)
     units = len(order)
-    held = refs[10 : 10 + units]
-    (x_sems, own_sems, up_sems, down_sems, piece_sems, far_sems, relay_sems, row_sems) = refs[10 + units :]
+    held = refs[15 : 16 + units]
+    (x_sems, own_sems, up_sems, down_sems, piece_sems, far_sems, relay_sems, row_sems, raw_sems) = refs[16 + units :]
 
     extent = bank_ref.shape[3]
     half = extent // 2
@@ -85,6 +85,24 @@
             device_id_type=pl.DeviceIdType.MESH,
         )
 
+    early = chunks - 1
+    last = sections - 1
+    extra = units
+
+    def raw_block():
+        return remote(bank_ref.at[0, last], held[extra].at[core, chip], raw_sems, (0,), {"sec": after})
+
+    def raw_names():
+        return remote(names, named, raw_sems, (1,), {"sec": after})
+
+    def raw_rows():
+        return remote(
+            x_ref.at[pl.ds(last * extent, extent), pl.ds(early * width, width)], raw, raw_sems, (2,), {"sec": after}
+        )
+
+    raw_block().start()
+    raw_rows().start()
+
     part = rows // PIECES
     first_number, first_k = order[0]
 
@@ -128,10 +146,13 @@
                     pl.when(has_down)(lambda: pass_down(src, high, step + 1, p).start())
                 pass_pair(src, high, chips + step, p).start()
 
+    for p in range(count):
+        names[p : p + 1, :] = jnp.full((1, extent), table_ref[0, last, p].astype(jnp.float32))
+    raw_names().start()
+
     def far(u, d):
-        number, k = order[u]
         return remote(
-            bank_ref.at[number, k],
+            held[extra].at[core, chip] if u == extra else bank_ref.at[order[u]],
             held[u].at[core, chip],
             far_sems,
             (u, d - 1),
@@ -140,7 +161,7 @@
 
     def far_arrival(u, d):
         return remote(
-            bank_ref.at[order[u]],
+            bank_ref.at[0, 0],
             held[u].at[core, lax.rem(chip + chips - d, chips)],
             far_sems,
             (u, d - 1),
@@ -175,12 +196,16 @@
         pass_pair(held[0].at[1 - core, chip, piece(p)], chip, 0, p).wait_recv()
     order_rows(0)
 
-    def receive(u):
+    def collect(u):
         for d in range(1, chips):
             far_arrival(u, d).wait_recv()
-        own(u).wait()
+        if u != extra:
+            own(u).wait()
         relay(u, core).start()
         relay(u, 1 - core).wait_recv()
+
+    def receive(u):
+        collect(u)
         order_rows(u)
 
     def split(value):
@@ -213,21 +238,21 @@
             {"sec": before},
         )
 
-    def each_chunk(body):
-        lax.fori_loop(0, chunks, lambda c, _: (body(c), 0)[1], 0)
-
-    last = sections - 1
+    def each_chunk(body, stop=chunks):
+        lax.fori_loop(0, stop, lambda c, _: (body(c), 0)[1], 0)
+
 
     def begin(c):
         load(c, last).wait()
         parts = split(xs[c, half + last * extent : top])
         u = index[0, last]
         sa[c, top - half : top] = product(u, half, half, parts)
-        forward(c, 0, sa).start()
+        pl.when(c != early)(lambda: forward(c, 0, sa).start())
         sa[c, half + last * extent : top - half] = product(u, 0, half, parts)
 
     each_chunk(begin)
-    for u in range(1, units):
+    raw_block().wait_recv()
+    for u in (1, 2, extra, *range(3, units)):
         for d in range(1, chips):
             far(u, d).start()
 
@@ -245,14 +270,29 @@
     receive(index[1, 0])
 
     def straddle(c):
-        forward(c, 0, sa).wait_recv()
+        pl.when(c != early)(lambda: forward(c, 0, sa).wait_recv())
         parts = split(sa[c, 0:extent])
         u = index[1, 0]
         rs[c] = product(u, 0, half, parts)
         back_first(c).start()
         sb[c, 0:half] = product(u, half, half, parts)
 
-    each_chunk(straddle)
+    each_chunk(straddle, early)
+
+    collect(extra)
+    raw_names().wait_recv()
+    raw_rows().wait_recv()
+    for b in range(count // 2, count):
+        block = jnp.zeros((rows, extent), jnp.float32)
+        for p in range(count):
+            number_of = jnp.broadcast_to(named[p : p + 1, :], (rows, extent))
+            block = jnp.where(number_of == float(b), held[extra][p % 2, p // 2], block)
+        at = (b - count // 2) * rows
+        ahi[at : at + rows, :], alo[at : at + rows, :] = split(block)
+    dot = functools.partial(jnp.dot, preferred_element_type=jnp.float32)
+    high, low = split(raw[...])
+    sa[early, 0:half] = dot(ahi[...], high) + (dot(ahi[...], low) + dot(alo[...], high))
+    straddle(early)
     for k in range(1, sections):
         receive(index[1, k])
 
@@ -298,7 +338,7 @@
     each_chunk(finish)
 
     def drain(c):
-        forward(c, 0, sa).wait_send()
+        pl.when(c != early)(lambda: forward(c, 0, sa).wait_send())
         back_first(c).wait_send()
         forward(c, 2, xs).wait_send()
         back_last(c).wait_send()
@@ -325,10 +365,13 @@
                     )
                 pass_pair(held[0].at[core, high, piece(p)], high, chips + step, p).wait_send()
 
-    for u in range(1, units):
+    for u in range(1, units + 1):
         for d in range(1, chips):
             far(u, d).wait_send()
         relay(u, core).wait_send()
+    raw_block().wait_send()
+    raw_names().wait_send()
+    raw_rows().wait_send()
     each_chunk(drain)
 
 
@@ -357,18 +400,24 @@
             pltpu.VMEM((chunks, half, width), f32),
             pltpu.VMEM((units, extent, extent), bf16),
             pltpu.VMEM((units, extent, extent), bf16),
-            *[pltpu.VMEM((2, chips, rows, extent), f32) for _ in range(units)],
+            pltpu.VMEM((extent, width), f32),
+            pltpu.VMEM((count, extent), f32),
+            pltpu.VMEM((count, extent), f32),
+            pltpu.VMEM((half, extent), bf16),
+            pltpu.VMEM((half, extent), bf16),
+            *[pltpu.VMEM((2, chips, rows, extent), f32) for _ in range(units + 1)],
             dma((sections, chunks)),
             dma((units,)),
             dma((2, chips - 1, PIECES)),
             dma((2, chips - 1, PIECES)),
             dma((2, 2 * chips - 1, PIECES)),
-            dma((2, units, chips - 1)),
-            dma((2, units)),
+            dma((2, units + 1, chips - 1)),
+            dma((2, units + 1)),
             dma((2, 4, chunks)),
+            dma((2, 3)),
         ],
         compiler_params=pltpu.CompilerParams(
-            collective_id=0, has_side_effects=True, vmem_limit_bytes=50 << 20
+            collective_id=0, has_side_effects=True, vmem_limit_bytes=54 << 20
         ),
         name="strip",
     )(owner_table, matrix_rows, factor_bank)

time: 205 us -> 201 us (0.980)
  Pallas kernels: 201 us -> 197 us
    pallas_call x1, Pallas kernels: 201 us -> 197 us  [local(): pl.pallas_call(functools.partial(strip_kernel, nsec, count, chunks, width...]
where the time goes in v3:
time: 201 us; the launch traced here: 200 us
  Pallas kernels  197 us (98%)
  local copies, waits for them, and re-layouts  3.4 us (2%)
    pallas_call x1, Pallas kernels, local(): pl.pallas_call(functools.partial(strip_kernel, nsec, count, chunks, width...  197 us

profile of v3, /device:TPU:0, one launch (start us, length us, event | category | flops | bytes accessed | tf_op | source)
XLA Modules:
  0.0 200.0 jit_solution(18285134044238293078)
XLA Ops:
  0.0 196.6 %strip.1 = f32[1024,2048]{1,0:T(8,128)S(1)} custom-call(s32[4,2,8]{2,1,0:T(2,128)} %refs_0_.1, f32[1024,2048]{1,0:T(8,128)} %refs_1_.1, f32[4,2,64,512]{3,2,1,0:T(8,128)} %refs_2_.1), custom_call_target="tpu_custom_call" | custom-call | tf_op jit(solution)/shard_map/strip/pallas_call | solution.py:387
  196.6 3.4 %copy.5 = f32[1024,2048]{1,0:T(8,128)} copy(f32[1024,2048]{1,0:T(8,128)S(1)} %strip.1) | data formatting | bytes 16777216

commit v4 on v3

--- a/solution.py
+++ b/solution.py
@@ -10,6 +10,7 @@
 ROUNDS = 4
 WIDTH = 256
 PIECES = 2
+AHEAD = 3
 
 
 def unit_order(sections):
@@ -23,13 +24,13 @@
 
 
 def strip_kernel(nsec, count, chunks, width, *refs):
-    table_ref, x_ref, bank_ref, out_ref = refs[:4]
-    xs, sa, sb, rs, ghi, glo, raw, names, named, ahi, alo = refs[4:15]
+    owners_ref, x_ref, bank_ref, out_ref = refs[:4]
+    xs, sa, sb, rs, ghi, glo, raw, names, named, ahi, alo, table_ref = refs[4:16]
     sections = bank_ref.shape[1]
     order = unit_order(sections)
     units = len(order)
-    held = refs[15 : 16 + units]
-    (x_sems, own_sems, up_sems, down_sems, piece_sems, far_sems, relay_sems, row_sems, raw_sems) = refs[16 + units :]
+    held = refs[16 : 17 + units]
+    (x_sems, own_sems, up_sems, down_sems, piece_sems, far_sems, relay_sems, row_sems, raw_sems, table_sem) = refs[17 + units :]
 
     extent = bank_ref.shape[3]
     half = extent // 2
@@ -57,11 +58,6 @@
         number, k = order[u]
         return pltpu.make_async_copy(bank_ref.at[number, k], held[u].at[core, chip], own_sems.at[u])
 
-    for k in range(sections - 1, -1, -1):
-        lax.fori_loop(0, chunks, lambda c, _, k=k: (load(c, k).start(), 0)[1], 0)
-    for u in range(units):
-        own(u).start()
-
     barrier = pltpu.get_barrier_semaphore()
 
     def greet(target):
@@ -73,6 +69,12 @@
     greet({"col": partner})
     pl.when(has_up)(lambda: greet({"col": (chip + 1) * 2 + core}))
     pl.when(has_down)(lambda: greet({"col": (chip - 1) * 2 + core}))
+    table = pltpu.make_async_copy(owners_ref, table_ref, table_sem)
+    table.start()
+    for k in range(sections - 1, -1, -1):
+        lax.fori_loop(0, chunks, lambda c, _, k=k: (load(c, k).start(), 0)[1], 0)
+    for u in range(units):
+        own(u).start()
     pl.semaphore_wait(barrier, 3 + has_up.astype(jnp.int32) + has_down.astype(jnp.int32))
 
     def remote(src, dst, sems, at, target):
@@ -146,6 +148,7 @@
                     pl.when(has_down)(lambda: pass_down(src, high, step + 1, p).start())
                 pass_pair(src, high, chips + step, p).start()
 
+    table.wait()
     for p in range(count):
         names[p : p + 1, :] = jnp.full((1, extent), table_ref[0, last, p].astype(jnp.float32))
     raw_names().start()
@@ -238,8 +241,8 @@
             {"sec": before},
         )
 
-    def each_chunk(body, stop=chunks):
-        lax.fori_loop(0, stop, lambda c, _: (body(c), 0)[1], 0)
+    def each_chunk(body, start=0, stop=chunks):
+        lax.fori_loop(start, stop, lambda c, _: (body(c), 0)[1], 0)
 
 
     def begin(c):
@@ -250,11 +253,16 @@
         pl.when(c != early)(lambda: forward(c, 0, sa).start())
         sa[c, half + last * extent : top - half] = product(u, 0, half, parts)
 
-    each_chunk(begin)
+    def send_far(*chosen):
+        for u in chosen:
+            for d in range(1, chips):
+                far(u, d).start()
+
+    each_chunk(begin, 0, AHEAD)
+    send_far(1, 2)
+    each_chunk(begin, AHEAD)
     raw_block().wait_recv()
-    for u in (1, 2, extra, *range(3, units)):
-        for d in range(1, chips):
-            far(u, d).start()
+    send_far(extra, *range(3, units))
 
     for k in range(last - 1, -1, -1):
         receive(index[0, k])
@@ -277,7 +285,7 @@
         back_first(c).start()
         sb[c, 0:half] = product(u, half, half, parts)
 
-    each_chunk(straddle, early)
+    each_chunk(straddle, stop=early)
 
     collect(extra)
     raw_names().wait_recv()
@@ -388,7 +396,7 @@
         functools.partial(strip_kernel, nsec, count, chunks, width),
         out_shape=pltpu.VMEM(matrix_rows.shape, matrix_rows.dtype),
         in_specs=[
-            pl.BlockSpec(memory_space=pltpu.SMEM),
+            pl.BlockSpec(memory_space=pl.ANY),
             pl.BlockSpec(memory_space=pl.ANY),
             pl.BlockSpec(memory_space=pl.ANY),
         ],
@@ -405,6 +413,7 @@
             pltpu.VMEM((count, extent), f32),
             pltpu.VMEM((half, extent), bf16),
             pltpu.VMEM((half, extent), bf16),
+            pltpu.SMEM((ROUNDS, sections, count), jnp.int32),
             *[pltpu.VMEM((2, chips, rows, extent), f32) for _ in range(units + 1)],
             dma((sections, chunks)),
             dma((units,)),
@@ -415,6 +424,7 @@
             dma((2, units + 1)),
             dma((2, 4, chunks)),
             dma((2, 3)),
+            dma(()),
         ],
         compiler_params=pltpu.CompilerParams(
             collective_id=0, has_side_effects=True, vmem_limit_bytes=54 << 20

time: 201 us -> 199 us (0.990)
  no operation moved by 1% of the time
where the time goes in v4:
time: 199 us
  Pallas kernels  195 us (98%)
  local copies, waits for them, and re-layouts  3.4 us (2%)
    pallas_call x1, Pallas kernels, local(): pl.pallas_call(functools.partial(strip_kernel, nsec, count, chunks, width...  195 us

profile of v4, /device:TPU:0, one launch (start us, length us, event | category | flops | bytes accessed | tf_op | source)
XLA Modules:
  0.0 198.7 jit_solution(11558179108970884615)
XLA Ops:
  0.0 195.3 %strip.1 = f32[1024,2048]{1,0:T(8,128)S(1)} custom-call(s32[4,2,8]{2,1,0:T(2,128)} %refs_0_.1, f32[1024,2048]{1,0:T(8,128)} %refs_1_.1, f32[4,2,64,512]{3,2,1,0:T(8,128)} %refs_2_.1), custom_call_target="tpu_custom_call" | custom-call | tf_op jit(solution)/shard_map/strip/pallas_call | solution.py:395
  195.3 3.4 %copy.5 = f32[1024,2048]{1,0:T(8,128)} copy(f32[1024,2048]{1,0:T(8,128)S(1)} %strip.1) | data formatting | bytes 16777216

commit v5 on v4

--- a/solution.py
+++ b/solution.py
@@ -30,7 +30,8 @@
     order = unit_order(sections)
     units = len(order)
     held = refs[16 : 17 + units]
-    (x_sems, own_sems, up_sems, down_sems, piece_sems, far_sems, relay_sems, row_sems, raw_sems, table_sem) = refs[17 + units :]
+    (x_sems, own_sem, line_sends, line_sems, pair_sem, far_send, far_sems, relay_send, relay_sems) = refs[17 + units : 26 + units]
+    (row_sends, row_sems, return_sem, raw_sends, raw_sems, table_sem) = refs[26 + units :]
 
     extent = bank_ref.shape[3]
     half = extent // 2
@@ -51,12 +52,12 @@
         return pltpu.make_async_copy(
             x_ref.at[pl.ds(k * extent, extent), columns(c)],
             xs.at[c, pl.ds(half + k * extent, extent)],
-            x_sems.at[k, c],
+            x_sems.at[k],
         )
 
     def own(u):
         number, k = order[u]
-        return pltpu.make_async_copy(bank_ref.at[number, k], held[u].at[core, chip], own_sems.at[u])
+        return pltpu.make_async_copy(bank_ref.at[number, k], held[u].at[core, chip], own_sem)
 
     barrier = pltpu.get_barrier_semaphore()
 
@@ -77,12 +78,18 @@
         own(u).start()
     pl.semaphore_wait(barrier, 3 + has_up.astype(jnp.int32) + has_down.astype(jnp.int32))
 
-    def remote(src, dst, sems, at, target):
+    def settle(ref, sem):
+        pltpu.make_async_copy(ref, ref, sem).wait()
+
+    def settle_blocks(blocks, sem):
+        settle(sb.at[:, pl.ds(0, blocks * rows * extent // (chunks * width))], sem)
+
+    def remote(src, dst, send_sem, recv_sem, target):
         return pltpu.make_async_remote_copy(
             src_ref=src,
             dst_ref=dst,
-            send_sem=sems.at[(0, *at)],
-            recv_sem=sems.at[(1, *at)],
+            send_sem=send_sem,
+            recv_sem=recv_sem,
             device_id=target,
             device_id_type=pl.DeviceIdType.MESH,
         )
@@ -92,14 +99,18 @@
     extra = units
 
     def raw_block():
-        return remote(bank_ref.at[0, last], held[extra].at[core, chip], raw_sems, (0,), {"sec": after})
+        return remote(bank_ref.at[0, last], held[extra].at[core, chip], raw_sends.at[0], raw_sems.at[0], {"sec": after})
 
     def raw_names():
-        return remote(names, named, raw_sems, (1,), {"sec": after})
+        return remote(names, named, raw_sends.at[1], raw_sems.at[1], {"sec": after})
 
     def raw_rows():
         return remote(
-            x_ref.at[pl.ds(last * extent, extent), pl.ds(early * width, width)], raw, raw_sems, (2,), {"sec": after}
+            x_ref.at[pl.ds(last * extent, extent), pl.ds(early * width, width)],
+            raw,
+            raw_sends.at[2],
+            raw_sems.at[2],
+            {"sec": after},
         )
 
     raw_block().start()
@@ -111,23 +122,26 @@
     def piece(p):
         return pl.ds(p * part, part)
 
-    def pass_up(src, slot, step, p):
-        return remote(src, held[0].at[core, slot, piece(p)], up_sems, (step, p), {"col": (chip + 1) * 2 + core})
-
-    def pass_down(src, slot, step, p):
-        return remote(src, held[0].at[core, slot, piece(p)], down_sems, (step, p), {"col": (chip - 1) * 2 + core})
-
-    def pass_pair(src, slot, step, p):
-        return remote(src, held[0].at[core, slot, piece(p)], piece_sems, (step, p), {"col": partner})
+    def passed(src, slot, p, way, target):
+        return remote(src, held[0].at[core, slot, piece(p)], line_sends.at[way], line_sems.at[slot, p], {"col": target})
+
+    def pass_up(src, slot, p):
+        return passed(src, slot, p, 0, (chip + 1) * 2 + core)
+
+    def pass_down(src, slot, p):
+        return passed(src, slot, p, 1, (chip - 1) * 2 + core)
+
+    def pass_pair(src, slot, p):
+        return remote(src, held[0].at[core, slot, piece(p)], line_sends.at[2], pair_sem, {"col": partner})
 
     def own_piece(p):
         return bank_ref.at[first_number, first_k, piece(p)]
 
     for p in range(PIECES):
-        pl.when(has_up)(lambda p=p: pass_up(own_piece(p), chip, 0, p).start())
-        pl.when(has_down)(lambda p=p: pass_down(own_piece(p), chip, 0, p).start())
+        pl.when(has_up)(lambda p=p: pass_up(own_piece(p), chip, p).start())
+        pl.when(has_down)(lambda p=p: pass_down(own_piece(p), chip, p).start())
     for p in range(PIECES):
-        pass_pair(own_piece(p), chip, 0, p).start()
+        pass_pair(own_piece(p), chip, p).start()
     for step in range(chips - 1):
         low, high = chip - 1 - step, chip + 1 + step
         for p in range(PIECES):
@@ -135,18 +149,18 @@
             @pl.when(low >= 0)
             def _(step=step, p=p, low=low):
                 src = held[0].at[core, low, piece(p)]
-                pass_up(src, low, step, p).wait_recv()
+                pass_up(src, low, p).wait_recv()
                 if step + 1 < chips - 1:
-                    pl.when(has_up)(lambda: pass_up(src, low, step + 1, p).start())
-                pass_pair(src, low, 1 + step, p).start()
+                    pl.when(has_up)(lambda: pass_up(src, low, p).start())
+                pass_pair(src, low, p).start()
 
             @pl.when(high < chips)
             def _(step=step, p=p, high=high):
                 src = held[0].at[core, high, piece(p)]
-                pass_down(src, high, step, p).wait_recv()
+                pass_down(src, high, p).wait_recv()
                 if step + 1 < chips - 1:
-                    pl.when(has_down)(lambda: pass_down(src, high, step + 1, p).start())
-                pass_pair(src, high, chips + step, p).start()
+                    pl.when(has_down)(lambda: pass_down(src, high, p).start())
+                pass_pair(src, high, p).start()
 
     table.wait()
     for p in range(count):
@@ -157,22 +171,16 @@
         return remote(
             held[extra].at[core, chip] if u == extra else bank_ref.at[order[u]],
             held[u].at[core, chip],
-            far_sems,
-            (u, d - 1),
+            far_send,
+            far_sems.at[u - 1],
             {"col": lax.rem(chip + d, chips) * 2 + core},
         )
 
-    def far_arrival(u, d):
-        return remote(
-            bank_ref.at[0, 0],
-            held[u].at[core, lax.rem(chip + chips - d, chips)],
-            far_sems,
-            (u, d - 1),
-            {"col": partner},
-        )
+    turns = []
 
     def relay(u, side):
-        return remote(held[u].at[side], held[u].at[side], relay_sems, (u,), {"col": partner})
+        at = turns.index(u) % 2
+        return remote(held[u].at[side], held[u].at[side], relay_send, relay_sems.at[at], {"col": partner})
 
     def order_rows(u):
         number, k = order[u]
@@ -185,25 +193,13 @@
             ghi[u, b * rows : (b + 1) * rows, :] = high
             glo[u, b * rows : (b + 1) * rows, :] = (block - high.astype(jnp.float32)).astype(jnp.bfloat16)
 
-    own(0).wait()
-    for step in range(chips - 1):
-        low, high = chip - 1 - step, chip + 1 + step
-        for p in range(PIECES):
-            pl.when(low >= 0)(
-                lambda: pass_pair(held[0].at[1 - core, low, piece(p)], low, 1 + step, p).wait_recv()
-            )
-            pl.when(high < chips)(
-                lambda: pass_pair(held[0].at[1 - core, high, piece(p)], high, chips + step, p).wait_recv()
-            )
-    for p in range(PIECES):
-        pass_pair(held[0].at[1 - core, chip, piece(p)], chip, 0, p).wait_recv()
+    settle(bank_ref, own_sem)
+    settle(held[0].at[1 - core], pair_sem)
     order_rows(0)
 
     def collect(u):
-        for d in range(1, chips):
-            far_arrival(u, d).wait_recv()
-        if u != extra:
-            own(u).wait()
+        turns.append(u)
+        settle(held[u].at[core, pl.ds(0, chips - 1)], far_sems.at[u - 1])
         relay(u, core).start()
         relay(u, 1 - core).wait_recv()
 
@@ -226,18 +222,28 @@
 
     def forward(c, which, buf):
         return remote(
-            buf.at[c, pl.ds(top - half, half)], buf.at[c, pl.ds(0, half)], row_sems, (which, c), {"sec": after}
+            buf.at[c, pl.ds(top - half, half)],
+            buf.at[c, pl.ds(0, half)],
+            row_sends.at[which],
+            row_sems.at[0, c],
+            {"sec": after},
         )
 
     def back_first(c):
-        return remote(rs.at[c], sb.at[c, pl.ds(local_rows - half, half)], row_sems, (1, c), {"sec": before})
+        return remote(
+            rs.at[c],
+            sb.at[c, pl.ds(local_rows - half, half)],
+            row_sends.at[1],
+            row_sems.at[1, c],
+            {"sec": before},
+        )
 
     def back_last(c):
         return remote(
             sa.at[c, pl.ds(0, half)],
             out_ref.at[pl.ds(local_rows - half, half), columns(c)],
-            row_sems,
-            (3, c),
+            row_sends.at[3],
+            return_sem,
             {"sec": before},
         )
 
@@ -245,8 +251,9 @@
         lax.fori_loop(start, stop, lambda c, _: (body(c), 0)[1], 0)
 
 
+    settle(xs.at[:, pl.ds(half + last * extent, extent)], x_sems.at[last])
+
     def begin(c):
-        load(c, last).wait()
         parts = split(xs[c, half + last * extent : top])
         u = index[0, last]
         sa[c, top - half : top] = product(u, half, half, parts)
@@ -266,9 +273,9 @@
 
     for k in range(last - 1, -1, -1):
         receive(index[0, k])
+        settle(xs.at[:, pl.ds(half + k * extent, extent)], x_sems.at[k])
 
         def inner(c, k=k):
-            load(c, k).wait()
             at = half + k * extent
             parts = split(xs[c, at : at + extent])
             sa[c, at : at + extent] = product(index[0, k], 0, extent, parts)
@@ -345,42 +352,23 @@
 
     each_chunk(finish)
 
-    def drain(c):
-        pl.when(c != early)(lambda: forward(c, 0, sa).wait_send())
-        back_first(c).wait_send()
-        forward(c, 2, xs).wait_send()
-        back_last(c).wait_send()
-        back_last(c).wait_recv()
-
-    for p in range(PIECES):
-        pass_pair(own_piece(p), chip, 0, p).wait_send()
-        pl.when(has_up)(lambda p=p: pass_up(own_piece(p), chip, 0, p).wait_send())
-        pl.when(has_down)(lambda p=p: pass_down(own_piece(p), chip, 0, p).wait_send())
-        for step in range(chips - 1):
-            low, high = chip - 1 - step, chip + 1 + step
-
-            @pl.when(low >= 0)
-            def _():
-                if step + 1 < chips - 1:
-                    pl.when(has_up)(lambda: pass_up(held[0].at[core, low, piece(p)], low, step + 1, p).wait_send())
-                pass_pair(held[0].at[core, low, piece(p)], low, 1 + step, p).wait_send()
-
-            @pl.when(high < chips)
-            def _():
-                if step + 1 < chips - 1:
-                    pl.when(has_down)(
-                        lambda: pass_down(held[0].at[core, high, piece(p)], high, step + 1, p).wait_send()
-                    )
-                pass_pair(held[0].at[core, high, piece(p)], high, chips + step, p).wait_send()
-
-    for u in range(1, units + 1):
-        for d in range(1, chips):
-            far(u, d).wait_send()
-        relay(u, core).wait_send()
+    for v in range(chips):
+        if v + 1 < chips:
+            pl.when(chip == v)(lambda: settle(held[0].at[core, pl.ds(0, v + 1)], line_sends.at[0]))
+        if v > 0:
+            pl.when(chip == v)(lambda: settle(held[0].at[core, pl.ds(0, chips - v)], line_sends.at[1]))
+    settle(held[0].at[core], line_sends.at[2])
+    settle_blocks(units * (chips - 1), far_send)
+    settle_blocks(units * chips, relay_send)
     raw_block().wait_send()
     raw_names().wait_send()
     raw_rows().wait_send()
-    each_chunk(drain)
+    if early:
+        settle(sa.at[pl.ds(0, early), pl.ds(top - half, half)], row_sends.at[0])
+    settle(rs, row_sends.at[1])
+    settle(xs.at[:, pl.ds(top - half, half)], row_sends.at[2])
+    settle(sa.at[:, pl.ds(0, half)], row_sends.at[3])
+    settle(out_ref.at[pl.ds(local_rows - half, half)], return_sem)
 
 
 def local(matrix_rows, factor_bank, owner_table):
@@ -415,15 +403,20 @@
             pltpu.VMEM((half, extent), bf16),
             pltpu.SMEM((ROUNDS, sections, count), jnp.int32),
             *[pltpu.VMEM((2, chips, rows, extent), f32) for _ in range(units + 1)],
-            dma((sections, chunks)),
+            dma((sections,)),
+            dma(()),
+            dma((3,)),
+            dma((chips, PIECES)),
+            dma(()),
+            dma(()),
             dma((units,)),
-            dma((2, chips - 1, PIECES)),
-            dma((2, chips - 1, PIECES)),
-            dma((2, 2 * chips - 1, PIECES)),
-            dma((2, units + 1, chips - 1)),
-            dma((2, units + 1)),
-            dma((2, 4, chunks)),
-            dma((2, 3)),
+            dma(()),
+            dma((2,)),
+            dma((4,)),
+            dma((2, chunks)),
+            dma(()),
+            dma((3,)),
+            dma((3,)),
             dma(()),
         ],
         compiler_params=pltpu.CompilerParams(

time: 199 us -> 197 us (0.990)
  no operation moved by 1% of the time
where the time goes in v5:
time: 197 us
  Pallas kernels  194 us (98%)
  local copies, waits for them, and re-layouts  3.4 us (2%)
    pallas_call x1, Pallas kernels, local(): pl.pallas_call(functools.partial(strip_kernel, nsec, count, chunks, width...  194 us

profile of v5, /device:TPU:0, one launch (start us, length us, event | category | flops | bytes accessed | tf_op | source)
XLA Modules:
  0.0 197.2 jit_solution(2611939002751452740)
XLA Ops:
  0.0 193.8 %strip.1 = f32[1024,2048]{1,0:T(8,128)S(1)} custom-call(s32[4,2,8]{2,1,0:T(2,128)} %refs_0_.1, f32[1024,2048]{1,0:T(8,128)} %refs_1_.1, f32[4,2,64,512]{3,2,1,0:T(8,128)} %refs_2_.1), custom_call_target="tpu_custom_call" | custom-call | tf_op jit(solution)/shard_map/strip/pallas_call | solution.py:383
  193.8 3.4 %copy.5 = f32[1024,2048]{1,0:T(8,128)} copy(f32[1024,2048]{1,0:T(8,128)S(1)} %strip.1) | data formatting | bytes 16777216

commit v6 on v5

--- a/solution.py
+++ b/solution.py
@@ -114,7 +114,7 @@
         )
 
     raw_block().start()
-    raw_rows().start()
+    pl.when(core == 0)(lambda: raw_rows().start())
 
     part = rows // PIECES
     first_number, first_k = order[0]
@@ -161,6 +161,9 @@
                 if step + 1 < chips - 1:
                     pl.when(has_down)(lambda: pass_down(src, high, p).start())
                 pass_pair(src, high, p).start()
+
+            if step == 0 and p == 0:
+                pl.when(core == 1)(lambda: raw_rows().start())
 
     table.wait()
     for p in range(count):
@@ -257,7 +260,8 @@
         parts = split(xs[c, half + last * extent : top])
         u = index[0, last]
         sa[c, top - half : top] = product(u, half, half, parts)
-        pl.when(c != early)(lambda: forward(c, 0, sa).start())
+        pl.when((c == 1) & (core == 1))(lambda: forward(0, 0, sa).start())
+        pl.when((c != early) & ((c > 0) | (core == 0)))(lambda: forward(c, 0, sa).start())
         sa[c, half + last * extent : top - half] = product(u, 0, half, parts)
 
     def send_far(*chosen):

time: 197 us -> 197 us (level)
  no operation moved by 1% of the time
where the time goes in v6:
time: 197 us; the launch traced here: 196 us
  Pallas kernels  193 us (98%)
  local copies, waits for them, and re-layouts  3.4 us (2%)
    pallas_call x1, Pallas kernels, local(): pl.pallas_call(functools.partial(strip_kernel, nsec, count, chunks, width...  193 us

profile of v6, /device:TPU:0, one launch (start us, length us, event | category | flops | bytes accessed | tf_op | source)
XLA Modules:
  0.0 196.2 jit_solution(10791110089044719190)
XLA Ops:
  0.0 192.8 %strip.1 = f32[1024,2048]{1,0:T(8,128)S(1)} custom-call(s32[4,2,8]{2,1,0:T(2,128)} %refs_0_.1, f32[1024,2048]{1,0:T(8,128)} %refs_1_.1, f32[4,2,64,512]{3,2,1,0:T(8,128)} %refs_2_.1), custom_call_target="tpu_custom_call" | custom-call | tf_op jit(solution)/shard_map/strip/pallas_call | solution.py:387
  192.8 3.4 %copy.5 = f32[1024,2048]{1,0:T(8,128)} copy(f32[1024,2048]{1,0:T(8,128)S(1)} %strip.1) | data formatting | bytes 16777216

commit v7 on v6

--- a/solution.py
+++ b/solution.py
@@ -30,8 +30,8 @@
     order = unit_order(sections)
     units = len(order)
     held = refs[16 : 17 + units]
-    (x_sems, own_sem, line_sends, line_sems, pair_sem, far_send, far_sems, relay_send, relay_sems) = refs[17 + units : 26 + units]
-    (row_sends, row_sems, return_sem, raw_sends, raw_sems, table_sem) = refs[26 + units :]
+    (x_sems, own_sem, line_sends, line_sems, pair_sem, far_send, far_sems, relay_sems) = refs[17 + units : 25 + units]
+    (row_send, row_sems, return_sem, raw_sems, table_sem) = refs[25 + units :]
 
     extent = bank_ref.shape[3]
     half = extent // 2
@@ -99,16 +99,16 @@
     extra = units
 
     def raw_block():
-        return remote(bank_ref.at[0, last], held[extra].at[core, chip], raw_sends.at[0], raw_sems.at[0], {"sec": after})
+        return remote(bank_ref.at[0, last], held[extra].at[core, chip], row_send, raw_sems.at[0], {"sec": after})
 
     def raw_names():
-        return remote(names, named, raw_sends.at[1], raw_sems.at[1], {"sec": after})
+        return remote(names, named, table_sem, raw_sems.at[1], {"sec": after})
 
     def raw_rows():
         return remote(
             x_ref.at[pl.ds(last * extent, extent), pl.ds(early * width, width)],
             raw,
-            raw_sends.at[2],
+            row_send,
             raw_sems.at[2],
             {"sec": after},
         )
@@ -183,7 +183,7 @@
 
     def relay(u, side):
         at = turns.index(u) % 2
-        return remote(held[u].at[side], held[u].at[side], relay_send, relay_sems.at[at], {"col": partner})
+        return remote(held[u].at[side], held[u].at[side], far_send, relay_sems.at[at], {"col": partner})
 
     def order_rows(u):
         number, k = order[u]
@@ -227,7 +227,7 @@
         return remote(
             buf.at[c, pl.ds(top - half, half)],
             buf.at[c, pl.ds(0, half)],
-            row_sends.at[which],
+            row_send,
             row_sems.at[0, c],
             {"sec": after},
         )
@@ -236,7 +236,7 @@
         return remote(
             rs.at[c],
             sb.at[c, pl.ds(local_rows - half, half)],
-            row_sends.at[1],
+            row_send,
             row_sems.at[1, c],
             {"sec": before},
         )
@@ -245,7 +245,7 @@
         return remote(
             sa.at[c, pl.ds(0, half)],
             out_ref.at[pl.ds(local_rows - half, half), columns(c)],
-            row_sends.at[3],
+            row_send,
             return_sem,
             {"sec": before},
         )
@@ -362,16 +362,10 @@
         if v > 0:
             pl.when(chip == v)(lambda: settle(held[0].at[core, pl.ds(0, chips - v)], line_sends.at[1]))
     settle(held[0].at[core], line_sends.at[2])
-    settle_blocks(units * (chips - 1), far_send)
-    settle_blocks(units * chips, relay_send)
-    raw_block().wait_send()
+    settle_blocks(units * (2 * chips - 1), far_send)
+    sent = (early + 3 * chunks) * half * width + (rows + width) * extent
+    settle(xs.at[:, pl.ds(0, sent // (chunks * width))], row_send)
     raw_names().wait_send()
-    raw_rows().wait_send()
-    if early:
-        settle(sa.at[pl.ds(0, early), pl.ds(top - half, half)], row_sends.at[0])
-    settle(rs, row_sends.at[1])
-    settle(xs.at[:, pl.ds(top - half, half)], row_sends.at[2])
-    settle(sa.at[:, pl.ds(0, half)], row_sends.at[3])
     settle(out_ref.at[pl.ds(local_rows - half, half)], return_sem)
 
 
@@ -414,12 +408,10 @@
             dma(()),
             dma(()),
             dma((units,)),
-            dma(()),
             dma((2,)),
-            dma((4,)),
+            dma(()),
             dma((2, chunks)),
             dma(()),
-            dma((3,)),
             dma((3,)),
             dma(()),
         ],

time: 197 us -> 197 us (level)
  no operation moved by 1% of the time
where the time goes in v7:
time: 197 us; the launch traced here: 196 us
  Pallas kernels  193 us (98%)
  local copies, waits for them, and re-layouts  3.4 us (2%)
    pallas_call x1, Pallas kernels, local(): pl.pallas_call(functools.partial(strip_kernel, nsec, count, chunks, width...  193 us

profile of v7, /device:TPU:0, one launch (start us, length us, event | category | flops | bytes accessed | tf_op | source)
XLA Modules:
  0.0 196.1 jit_solution(1254560950163162516)
XLA Ops:
  0.0 192.7 %strip.1 = f32[1024,2048]{1,0:T(8,128)S(1)} custom-call(s32[4,2,8]{2,1,0:T(2,128)} %refs_0_.1, f32[1024,2048]{1,0:T(8,128)} %refs_1_.1, f32[4,2,64,512]{3,2,1,0:T(8,128)} %refs_2_.1), custom_call_target="tpu_custom_call" | custom-call | tf_op jit(solution)/shard_map/strip/pallas_call | solution.py:381
  192.7 3.4 %copy.5 = f32[1024,2048]{1,0:T(8,128)} copy(f32[1024,2048]{1,0:T(8,128)S(1)} %strip.1) | data formatting | bytes 16777216
